TPU v7x, 128 devices: a whole 4x4x4 slice. The times are simulated.
128 devices in a mesh: rows: 32 (over x, z, core), rel: 4 (over y).
Axes of the slice: x: 4, y: 4, z: 4, core: 2. Of those that a mesh axis runs over, the one named last changes fastest.
Arguments:
- features: bfloat16 [16384, 256], P('rows'), may hold values from -6 to 6
- bases: bfloat16 [8, 256, 256], replicated, may hold values from -0.125 to 0.125
- root: bfloat16 [256, 256], replicated, may hold values from -0.375 to 0.375
- coeffs: float32 [800, 8], P('rel'), may hold values from -4 to 4
- tiles: bfloat16 [32, 4, 64, 128, 128], P('rows', 'rel'), as said below
- tile_dst: int32 [32, 4, 64], P('rows', 'rel'), may hold values from 0 to 3
- tile_src: int32 [32, 4, 64], P('rows', 'rel'), may hold values from 0 to 63
- tile_rel: int32 [32, 4, 64], P('rows', 'rel'), may hold values from 0 to 199
- tile_live: int32 [32, 4], P('rows', 'rel'), may hold values from 16 to 64, as said below
- send_list: int32 [32, 4, 32, 2], P('rows', 'rel'), may hold values from 0 to 3
- cotangent: bfloat16 [16384, 256], P('rows'), may hold values from -6 to 6
Outputs:
- output: bfloat16 [16384, 256], P('rows')
- feature_grad: float32 [16384, 256], P('rows')
- basis_grad: float32 [8, 256, 256], replicated
- root_grad: float32 [256, 256], replicated
Inputs may be any that keep to these rules, and one draw needn't show every extreme that they name: `tile_live`: at least one device uses all 64 tile slots. `tiles`: entries are zero or positive, at most 12 / sqrt(2048).
All inputs are finite; a program needn't handle non-finite values.
Results may differ from a plain program's by a relative error of at most 0.0029.
Values may be sent and summed in bfloat16 or wider, within the bound.
A program may use at most 128 MiB of HBM per device.

v0:
```python
import math
import jax
import jax.numpy as jnp
from jax import lax
from jax.sharding import PartitionSpec as P


def on_device(
    features,
    bases,
    root,
    coeffs,
    tiles,
    tile_dst,
    tile_src,
    tile_rel,
    tile_live,
    send_list,
    cotangent,
):
    highest = lax.Precision.HIGHEST
    contract_first = (((0,), (0,)), ((), ()))
    feat_width = features.shape[1]
    size_block = tiles.shape[-1]
    blocks = features.reshape(-1, size_block, feat_width)
    local_blocks = blocks.shape[0]
    num_bases = bases.shape[0]
    slots_peer = send_list.shape[-1]
    row_devices = lax.axis_size("rows")
    total_slots = row_devices * slots_peer
    count_tiles = tiles.shape[2]
    adjacency = tiles[0, 0]
    dst_ids = tile_dst[0, 0]
    src_ids = tile_src[0, 0]
    rel_ids = tile_rel[0, 0]
    live_count = tile_live[0, 0]
    send_rows = send_list[0, 0]
    outgoing = blocks[send_rows]
    incoming = lax.all_to_all(outgoing, "rows", split_axis=0, concat_axis=0, tiled=True)
    received = incoming.reshape(total_slots, size_block, feat_width)
    step_tiles = math.gcd(count_tiles, 64)
    steps_live = (live_count + step_tiles - 1) // step_tiles

    def tile_weights(first_tile):
        position = first_tile + jnp.arange(step_tiles)
        in_use = (position < live_count).astype(jnp.float32)
        rel_hot = (rel_ids[:, None] == jnp.arange(coeffs.shape[0])[None, :]).astype(jnp.float32)
        coef_rows = jnp.dot(rel_hot, coeffs, precision=highest)
        dst_hot = (dst_ids[:, None] == jnp.arange(local_blocks)[None, :]).astype(
            jnp.float32
        ) * in_use[:, None]
        return (dst_hot[:, :, None] * coef_rows[:, None, :]).reshape(
            step_tiles, local_blocks * num_bases
        )

    def forward_step(block_index, running):
        first_tile = block_index * step_tiles
        sources = received[src_ids]
        messages = jnp.einsum(
            "tij,tjf->tif", adjacency, sources, preferred_element_type=jnp.float32
        )
        weights = tile_weights(first_tile)
        return running + lax.dot_general(
            weights, messages.reshape(step_tiles, -1), contract_first, precision=highest
        )

    zero_total = jnp.zeros((local_blocks * num_bases, size_block * feat_width), jnp.float32)
    partial_value = lax.fori_loop(0, steps_live, forward_step, zero_total)
    partial_value = partial_value.reshape(local_blocks, num_bases, size_block, feat_width)
    basis_f32 = bases.astype(jnp.float32)
    cot_blocks = cotangent.reshape(local_blocks, size_block, feat_width)
    cot_f32 = cot_blocks.astype(jnp.float32)
    root_term = jnp.dot(features, root, preferred_element_type=jnp.float32)
    root_local = lax.dot_general(
        features, cotangent, contract_first, preferred_element_type=jnp.float32
    )
    aggregate = lax.psum(partial_value, "rel")
    projected = jnp.einsum("lbnf,bfg->lng", aggregate, basis_f32, precision=highest)
    basis_local = jnp.einsum("lbnf,lng->bfg", aggregate, cot_f32, precision=highest)
    basis_grad, root_grad = lax.psum((basis_local, root_local), "rows")
    output = (projected.reshape(-1, feat_width) + root_term).astype(jnp.bfloat16)
    agg_grad = jnp.einsum("lng,bfg->lbnf", cot_blocks, bases, preferred_element_type=jnp.float32)
    agg_grad = agg_grad.reshape(local_blocks * num_bases, size_block * feat_width)

    def backward_step(block_index, running):
        first_tile = block_index * step_tiles
        weights = tile_weights(first_tile)
        spread = jnp.dot(weights, agg_grad, precision=highest).astype(jnp.bfloat16)
        spread = spread.reshape(step_tiles, size_block, feat_width)
        backward_term = jnp.einsum(
            "tij,tif->tjf", adjacency, spread, preferred_element_type=jnp.float32
        )
        slot_hot = (src_ids[:, None] == jnp.arange(total_slots)[None, :]).astype(jnp.float32)
        return running + lax.dot_general(
            slot_hot, backward_term.reshape(step_tiles, -1), contract_first, precision=highest
        )

    slot_zero = jnp.zeros((total_slots, size_block * feat_width), jnp.float32)
    slot_grads = lax.fori_loop(0, steps_live, backward_step, slot_zero)
    returned = lax.all_to_all(
        slot_grads.reshape(row_devices, slots_peer, size_block * feat_width),
        "rows",
        split_axis=0,
        concat_axis=0,
        tiled=True,
    )
    block_hot = (send_rows.reshape(-1)[None, :] == jnp.arange(local_blocks)[:, None]).astype(
        jnp.float32
    )
    own_grads = jnp.dot(block_hot, returned.reshape(total_slots, -1), precision=highest)
    summed = lax.psum(own_grads, "rel")
    root_back = lax.dot_general(
        cotangent, root, (((1,), (1,)), ((), ())), preferred_element_type=jnp.float32
    )
    feature_grad = summed.reshape(-1, feat_width) + root_back
    return (output, feature_grad, basis_grad, root_grad)


def solution(mesh):
    return jax.shard_map(
        on_device,
        mesh=mesh,
        in_specs=(
            P("rows", None),
            P(),
            P(),
            P("rel", None),
            P("rows", "rel", None, None, None),
            P("rows", "rel", None),
            P("rows", "rel", None),
            P("rows", "rel", None),
            P("rows", "rel"),
            P("rows", "rel", None, None),
            P("rows", None),
        ),
        out_specs=(P("rows", None), P("rows", None), P(), P()),
        check_vma=False,
    )
```

profile of v0, /device:TPU:1, one launch (start us, length us, event | category | flops | bytes accessed | tf_op | source)
XLA Modules:
  0.0 457.6 jit_solution(15787599625584917114)
XLA Ops:
  7.2 0.0 copy-start
  7.2 0.8 compare_select_fusion
  8.0 0.1 copy.23
  8.0 0.1 reshape.248
  8.2 3.7 gather_fusion
  11.9 0.0 copy-start.3
  11.9 9.6 %all-to-all-start = ((bf16[32,2,128,256]{3,2,1,0:T(8,128)(2,1)}), bf16[32,2,128,256]{3,2,1,0:T(8,128)(2,1)}, u32[]{:S(2)}, u32[]{:S(2)}) async-start(bf16[32,2,128,256]{3,2,1,0:T(8,128)(2,1)} %bitcast.130), calls=%async_computation | async-start | bytes 8388608 | tf_op jit(solution)/shard_map/all_to_all | solution.py:39
  22.2 0.0 copy-done
  22.2 0.0 copy-done.3
  22.2 2.7 convolution_bitcast_fusion.1
  24.9 0.0 copy-start.11
  24.9 5.5 %copy.36 = f32[4,8,128,256]{3,1,2,0:T(8,128)} copy(f32[4,8,128,256]{2,3,0,1:T(8,128)} %convolution_bitcast_fusion.1) | data formatting | bytes 8388608
  30.4 0.0 copy-done.11
  30.4 0.0 copy-done.12
  30.4 0.2 fusion.15
  30.6 0.0 copy-start.9
  30.6 3.9 broadcast_in_dim.5
  34.5 0.0 copy-done.1
  34.5 0.0 copy-done.8
  34.5 0.0 copy-done.9
  34.5 38.4 %while.25 = (s32[]{:T(128)}, f32[64,32768]{1,0:T(8,128)}, s32[]{:T(128)}, s32[1,1,64]{2,1,0:T(1,128)S(1)}, s32[1,1,64]{2,1,0:T(1,128)S(1)}, /*index=5*/s32[]{:T(...) while((s32[]{:T(128)}, f32[64,32768]{1,0:T(8,128)}, ...), condition=%wide.region_4.5_spmd, body=%wide.region_3.4_spmd.sunk | while | flops 2956991232 | bytes 73405568 | solution.py:99
  34.7 0.7 compare_convert_fusion.5
  35.4 8.6 %convolution_convert_fusion.2 = bf16[64,32768]{1,0:T(8,128)(2,1)S(1)} fusion(f32[32,32768]{1,0:T(8,128)} %get-tuple-element.440, f32[64,8]{0,1:T(8,128)S(1)} %get-tuple-element.439, f32[64,4]{0,1:T(4,128)S(1)} %fusion.64), kind=kOutput, calls=%fused_computation.11.clone.1 | convolution fusion | flops 807405568 | bytes 8391680 | tf_op jit(solution)/shard_map/while/body/dot_general | solution.py:88
  44.0 1.1 copy.45
  45.1 4.5 convolution_bitcast_fusion.4
  49.6 9.2 %copy.46 = f32[8,8,128,256]{3,1,2,0:T(8,128)} copy(f32[8,8,128,256]{2,3,1,0:T(8,128)} %bitcast.122) | data formatting | bytes 16777216 | tf_op jit(solution)/shard_map/while
  58.8 14.1 %convolution_add_fusion.7 = f32[64,32768]{1,0:T(8,128)} fusion(f32[64,32768]{1,0:T(8,128)} %get-tuple-element.423, f32[64,32768]{1,0:T(8,128)} %bitcast.121, s32[64]{0:T(128)S(1)} %bitcast.136), kind=kOutput, calls=%fused_computation.10.clone.1 | convolution fusion | flops 1612713984 | bytes 25166080 | tf_op jit(solution)/shard_map/while/body/dot_general | solution.py:94
  72.9 10.6 %reshape.243 = f32[32,2,32768]{2,1,0:T(2,128)} reshape(f32[64,32768]{1,0:T(8,128)} %get-tuple-element.236) | data formatting | bytes 16777216 | tf_op jit(solution)/shard_map/reshape | solution.py:101
  83.6 0.0 all-to-all-done
  83.6 7.6 %all-to-all-start.1 = ((f32[32,2,32768]{2,1,0:T(2,128)}), f32[32,2,32768]{2,1,0:T(2,128)}, u32[]{:S(2)}, u32[]{:S(2)}) async-start(f32[32,2,32768]{2,1,0:T(2,128)} %reshape.243), calls=%async_computation.1 | async-start | bytes 16777216 | tf_op jit(solution)/shard_map/all_to_all | solution.py:100
  91.1 0.0 all-reduce.7.cloned.1.call-start
  91.2 0.0 copy-done.10
  91.2 0.1 copy.24
  91.3 0.1 eq.116
  91.4 4.9 %gather_fusion.1 = bf16[64,128,256]{2,1,0:T(8,128)(2,1)} fusion(bf16[64,128,256]{2,1,0:T(8,128)(2,1)} %bitcast.12, s32[1024]{0:T(1024)S(1)} %pad_clamp_fusion), kind=kCustom, calls=%fused_computation.1 | custom fusion | bytes 8388864 | tf_op jit(solution)/shard_map/while/body/gather | solution.py:58
  96.3 2.3 broadcast_in_dim.4
  98.6 16.0 %while.24 = (s32[]{:T(128)}, f32[32,32768]{1,0:T(8,128)}, s32[]{:T(128)}, s32[1,1,64]{2,1,0:T(1,128)S(1)}, s32[]{:T(128)}, /*index=5*/f32[64,8]{0,1:T(8,128)S(1)...) while((s32[]{:T(128)}, f32[32,32768]{1,0:T(8,128)}, s32[]{:T(128)}, ...), condition=%wide.region_1.2_spmd, body=%wide.region_0.1_spmd.sunk | while | flops 1343228672 | bytes 48239480 | solution.py:68
  98.6 0.6 compare_convert_fusion.4
  99.3 3.4 fusion.57
  102.7 4.7 %copy.44 = f32[8,8,128,256]{3,1,2,0:T(8,128)S(1)} copy(f32[8,8,128,256]{3,2,1,0:T(8,128)S(1)} %bitcast.123) | data formatting | bytes 16777216 | tf_op jit(solution)/shard_map/while
  107.5 7.1 %convolution_add_fusion.6 = f32[32,32768]{1,0:T(8,128)} fusion(f32[32,32768]{1,0:T(8,128)} %get-tuple-element.392, f32[64,32768]{1,0:T(8,128)S(1)} %bitcast.120, f32[64,8]{0,1:T(8,128)S(1)} %get-tuple-element.406, f32[64,4]{0,1:T(4,128)S(1)} %fusion.58), kind=kOutput, calls=%fused_computation.2.clone.1 | convolution fusion | flops 806356992 | bytes 16780288 | tf_op jit(solution)/shard_map/while/body/dot_general | solution.py:63
  114.6 5.4 %copy.40 = f32[4,8,128,256]{3,2,1,0:T(8,128)} copy(f32[4,8,128,256]{3,1,2,0:T(8,128)} %bitcast.127) | data formatting | bytes 8388608
  120.0 78.3 %all-to-all-done.1 = f32[32,2,32768]{2,1,0:T(2,128)} async-done(((f32[32,2,32768]{2,1,0:T(2,128)}), f32[32,2,32768]{2,1,0:T(2,128)}, u32[]{:S(2)}, u32[]{:S(2)}) %all-to-all-start.1) | async-done | bytes 8388640 | tf_op jit(solution)/shard_map/all_to_all | solution.py:100
  198.3 10.9 %reshape.244 = f32[64,32768]{1,0:T(8,128)} reshape(f32[32,2,32768]{2,1,0:T(2,128)} %all-to-all-done.1) | data formatting | bytes 16777216 | tf_op jit(solution)/shard_map/reshape | solution.py:110
  209.3 6.2 %fusion.17 = f32[4,32768]{1,0:T(4,128)S(1)} fusion(f32[64,32768]{1,0:T(8,128)} %reshape.244, s32[64]{0:T(128)S(1)} %eq.116), kind=kOutput, calls=%fused_computation.39 | convolution fusion | flops 100663552 | bytes 8913152 | tf_op jit(solution)/shard_map/dot_general | solution.py:110
  215.5 0.0 copy-start.4
  215.5 1.2 reshape.245
  216.6 0.0 all-reduce.7.cloned.1.call-update
  216.6 0.0 all-reduce.5.cloned.1.call-start
  216.7 0.0 copy-done.2
  216.7 0.0 copy-done.4
  216.7 1.0 fusion.21
  217.7 114.5 %all-reduce.7.cloned.1.call-done = (f32[4,8,128,256]{3,2,1,0:T(8,128)}, f32[512,256]{1,0:T(8,128)}) async-done(((f32[4,8,128,256]{3,2,1,0:T(8,128)}, f32[512,256]{1,0:T(8,128)}), (f32[4,8,128,256]{3,2,1,0:T(8,128)}, f32[512,256]{1,0:T(8,128)})) %all-reduce.7.cloned.1.call-update) | async-done | bytes 4718608 | tf_op jit(solution)/shard_map/psum | solution.py:77
  332.1 6.9 %convolution_bitcast_fusion.2 = f32[8,256,256]{2,1,0:T(8,128)} fusion(f32[4,8,128,256]{3,2,1,0:T(8,128)} %get-tuple-element.273, bf16[4,128,256,1]{2,1,3,0:T(8,128)(2,1)S(1)} %bitcast.132), kind=kOutput, calls=%fused_computation.24 | convolution fusion | flops 3221225472 | bytes 6553600 | tf_op jit(solution)/shard_map/lbnf,lng->bfg/dot_general | solution.py:79
  339.1 0.0 all-reduce.5.cloned.1.call-update
  339.1 4.3 fusion.13
  343.4 0.0 copy-done.6
  343.4 0.9 fusion.11
  344.3 0.0 copy-done.5
  344.3 1.1 convolution_add_fusion.2
  345.4 101.6 %all-reduce.5.cloned.1.call-done = (f32[8,256,256]{2,1,0:T(8,128)}, f32[256,256]{1,0:T(8,128)}) async-done(((f32[8,256,256]{2,1,0:T(8,128)}, f32[256,256]{1,0:T(8,128)}), (f32[8,256,256]{2,1,0:T(8,128)}, f32[256,256]{1,0:T(8,128)})) %all-reduce.5.cloned.1.call-update) | async-done | bytes 2359312 | tf_op jit(solution)/shard_map/psum | solution.py:80
  447.0 3.1 copy.65
  450.1 0.0 copy-done.7
  450.1 0.7 copy.66
  (13 shorter events, 0.0 us)
Async XLA Ops:
  7.2 15.0 %copy-start = (bf16[8,256,256]{2,1,0:T(8,128)(2,1)S(1)}, bf16[8,256,256]{2,1,0:T(8,128)(2,1)}, u32[]{:S(2)}) copy-start(bf16[8,256,256]{2,1,0:T(8,128)(2,1)} %param.16) | copy-start | bytes 3145732
  11.9 10.3 %copy-start.3 = (bf16[512,256]{1,0:T(8,128)(2,1)S(1)}, bf16[512,256]{1,0:T(8,128)(2,1)}, u32[]{:S(2)}) copy-start(bf16[512,256]{1,0:T(8,128)(2,1)} %param.25) | copy-start | bytes 786436
  11.9 71.7 %all-to-all-start = ((bf16[32,2,128,256]{3,2,1,0:T(8,128)(2,1)}), bf16[32,2,128,256]{3,2,1,0:T(8,128)(2,1)}, u32[]{:S(2)}, u32[]{:S(2)}) async-start(bf16[32,2,128,256]{3,2,1,0:T(8,128)(2,1)} %bitcast.130), calls=%async_computation | async-start | bytes 8388608 | tf_op jit(solution)/shard_map/all_to_all | solution.py:39
  24.9 5.5 %copy-start.11 = (f32[200,8]{0,1:T(8,128)S(1)}, f32[200,8]{0,1:T(8,128)}, u32[]{:S(2)}) copy-start(f32[200,8]{0,1:T(8,128)} %param.18) | copy-start | bytes 19204
  24.9 5.5 %copy-start.12 = (s32[1,1,64]{2,1,0:T(1,128)S(1)}, s32[1,1,64]{2,1,0:T(1,128)}, u32[]{:S(2)}) copy-start(s32[1,1,64]{2,1,0:T(1,128)} %param.22) | copy-start | bytes 772
  30.6 4.0 copy-start.1
  30.6 4.0 copy-start.8
  30.6 4.0 copy-start.9
  83.6 7.6 %copy-start.10 = (s32[1,1,32,2]{2,3,1,0:T(2,128)S(1)}, s32[1,1,32,2]{2,3,1,0:T(2,128)}, u32[]{:S(2)}) copy-start(s32[1,1,32,2]{2,3,1,0:T(2,128)} %param.24) | copy-start | bytes 772
  83.6 114.8 %all-to-all-start.1 = ((f32[32,2,32768]{2,1,0:T(2,128)}), f32[32,2,32768]{2,1,0:T(2,128)}, u32[]{:S(2)}, u32[]{:S(2)}) async-start(f32[32,2,32768]{2,1,0:T(2,128)} %reshape.243), calls=%async_computation.1 | async-start | bytes 16777216 | tf_op jit(solution)/shard_map/all_to_all | solution.py:100
  91.1 241.0 %all-reduce.7.cloned.1.call-start = ((), (), s32[]{:S(2)}) async-start(), calls=%async_computation.3 | async-start | bytes 9437184 | tf_op jit(solution)/shard_map/psum | solution.py:77
  215.4 1.2 copy-start.2
  215.5 1.3 copy-start.4
  216.6 230.3 %all-reduce.5.cloned.1.call-start = ((), (), s32[]{:S(2)}) async-start(), calls=%async_computation.2 | async-start | bytes 4718592 | tf_op jit(solution)/shard_map/psum | solution.py:80
  339.1 4.3 copy-start.6
  339.1 5.2 %copy-start.5 = (f32[512,256]{1,0:T(8,128)S(1)}, f32[512,256]{1,0:T(8,128)}, u32[]{:S(2)}) copy-start(f32[512,256]{1,0:T(8,128)} %get-tuple-element.274) | copy-start | bytes 1572868
  447.0 3.1 copy-start.7
Sparse Core Ops, SparseCore 0:
  216.8 115.3 all-reduce.6
  339.2 107.6 all-reduce.4
where the time goes:
time: 459 us; the launch traced here: 458 us
  waiting for transfers between devices  294 us (64%)
  local copies, waits for them, and re-layouts  67.8 us (15%)
  matrix products  60.9 us (13%)
  starting transfers between devices  17.3 us (4%)
  between operations  14.8 us (3%)
    psum x1, waiting for transfers between devices, on_device(): aggregate = lax.psum(partial_value, 'rel')  114 us
    psum x1, waiting for transfers between devices, on_device(): basis_grad, root_grad = lax.psum((basis_local, root_local), 'rows')  102 us
    all_to_all x1, waiting for transfers between devices, on_device(): lax.all_to_all(slot_grads.reshape(row_devices, slots_peer, size_block * f...  78.3 us
    while x3, local copies, waits for them, and re-layouts  15 us
    unnamed x31, local copies, waits for them, and re-layouts  14.9 us
    dot_general x1, matrix products, backward_step(): lax.dot_general(slot_hot, backward_term.reshape(step_tiles, -1), contract...  14.1 us
    reshape x1, local copies, waits for them, and re-layouts, on_device(): returned.reshape(total_slots, -1)  10.9 us
    reshape x1, local copies, waits for them, and re-layouts, on_device(): slot_grads.reshape(row_devices, slots_peer, size_block * feat_width)  10.6 us
  transfers between devices with their start and end apart: 4, of which 3 were waited for; matrix products, arithmetic and copies ran while one was open for 21% of the time, Pallas kernels for 0%

commit v1 on v0

--- a/solution.py
+++ b/solution.py
@@ -74,7 +74,7 @@
     root_local = lax.dot_general(
         features, cotangent, contract_first, preferred_element_type=jnp.float32
     )
-    aggregate = lax.psum(partial_value, "rel")
+    aggregate = jnp.sum(lax.all_gather(partial_value, "rel"), axis=0)
     projected = jnp.einsum("lbnf,bfg->lng", aggregate, basis_f32, precision=highest)
     basis_local = jnp.einsum("lbnf,lng->bfg", aggregate, cot_f32, precision=highest)
     basis_grad, root_grad = lax.psum((basis_local, root_local), "rows")

time: 459 us -> 488 us (1.063); the launches traced: 458 us -> 479 us
  other arithmetic: 2.1 us -> 12 us
  local copies, waits for them, and re-layouts: 67.8 us -> 74.5 us
  waiting for transfers between devices: 294 us -> 299 us
    psum x1, waiting for transfers between devices: 114 us -> 37.4 us  [on_device(): summed = lax.psum(own_grads, 'rel')]
    all_to_all x1, waiting for transfers between devices: 0.01 us -> 51.2 us  [on_device(): lax.all_to_all(outgoing, 'rows', split_axis=0, concat_axis=0, tiled=True)]
    all_to_all x1, waiting for transfers between devices: 78.3 us -> 107 us  [on_device(): lax.all_to_all(slot_grads.reshape(row_devices, slots_peer, size_block * f...]
    reduce_sum x0 -> x1, other arithmetic: none -> 9.85 us  [on_device(): aggregate = jnp.sum(lax.all_gather(partial_value, 'rel'), axis=0)]
    unnamed x31 -> x27, local copies, waits for them, and re-layouts: 14.9 us -> 15.9 us
  transfers between devices with their start and end apart: 4 -> 5, of which waited for: 3 -> 4; matrix products, arithmetic and copies ran while one was open for 21% -> 23% of each run, Pallas kernels for 0% -> 0%
where the time goes in v1:
time: 488 us; the launch traced here: 479 us
  waiting for transfers between devices  299 us (61%)
  local copies, waits for them, and re-layouts  74.5 us (15%)
  matrix products  61.2 us (13%)
  starting transfers between devices  16.9 us (3%)
  between operations  14.9 us (3%)
  other arithmetic  12 us (2%)
    all_to_all x1, waiting for transfers between devices, on_device(): lax.all_to_all(slot_grads.reshape(row_devices, slots_peer, size_block * f...  107 us
    psum x1, waiting for transfers between devices, on_device(): basis_grad, root_grad = lax.psum((basis_local, root_local), 'rows')  104 us
    all_to_all x1, waiting for transfers between devices, on_device(): lax.all_to_all(outgoing, 'rows', split_axis=0, concat_axis=0, tiled=True)  51.2 us
    psum x1, waiting for transfers between devices, on_device(): summed = lax.psum(own_grads, 'rel')  37.4 us
    unnamed x27, local copies, waits for them, and re-layouts  15.9 us
    while x3, local copies, waits for them, and re-layouts  15.1 us
    dot_general x1, matrix products, backward_step(): lax.dot_general(slot_hot, backward_term.reshape(step_tiles, -1), contract...  14.1 us
    reshape x1, local copies, waits for them, and re-layouts, on_device(): returned.reshape(total_slots, -1)  10.9 us
  transfers between devices with their start and end apart: 5, of which 4 were waited for; matrix products, arithmetic and copies ran while one was open for 23% of the time, Pallas kernels for 0%

profile of v1, /device:TPU:1, one launch (start us, length us, event | category | flops | bytes accessed | tf_op | source)
XLA Modules:
  0.0 479.1 jit_solution(5645427993196151722)
XLA Ops:
  7.2 0.0 copy-start
  7.2 0.8 compare_select_fusion
  8.0 0.1 copy.36
  8.0 0.1 reshape.242
  8.2 3.7 gather_fusion
  11.9 0.0 copy-start.7
  11.9 0.0 copy-start.9
  11.9 9.6 %all-to-all-start = ((bf16[32,2,128,256]{3,2,1,0:T(8,128)(2,1)}), bf16[32,2,128,256]{3,2,1,0:T(8,128)(2,1)}, u32[]{:S(2)}, u32[]{:S(2)}) async-start(bf16[32,2,128,256]{3,2,1,0:T(8,128)(2,1)} %bitcast.130), calls=%async_computation | async-start | bytes 8388608 | tf_op jit(solution)/shard_map/all_to_all | solution.py:39
  21.5 0.0 all-gather.2.cloned.1.call-start
  22.2 0.0 copy-done.7
  22.3 0.0 copy-done.9
  22.3 0.0 copy-done.10
  22.3 0.2 fusion.18
  22.5 51.2 %all-to-all-done = bf16[32,2,128,256]{3,2,1,0:T(8,128)(2,1)} async-done(((bf16[32,2,128,256]{3,2,1,0:T(8,128)(2,1)}), bf16[32,2,128,256]{3,2,1,0:T(8,128)(2,1)}, u32[]{:S(2)}, u32[]{:S(2)}) %all-to-all-start) | async-done | bytes 4194336 | tf_op jit(solution)/shard_map/all_to_all | solution.py:39
  73.6 5.0 %gather_fusion.1 = bf16[64,128,256]{2,1,0:T(8,128)(2,1)} fusion(bf16[64,128,256]{2,1,0:T(8,128)(2,1)} %bitcast.12, s32[1024]{0:T(1024)S(1)} %pad_clamp_fusion), kind=kCustom, calls=%fused_computation.1 | custom fusion | bytes 8388864 | tf_op jit(solution)/shard_map/while/body/gather | solution.py:58
  78.6 2.3 broadcast_in_dim.4
  80.8 0.2 copy-done.1
  81.0 0.0 copy-done.6
  81.0 16.1 %while.24 = (s32[]{:T(128)}, f32[32,32768]{1,0:T(8,128)}, s32[]{:T(128)}, s32[1,1,64]{2,1,0:T(1,128)S(1)}, s32[]{:T(128)}, /*index=5*/f32[64,8]{0,1:T(8,128)S(1)...) while((s32[]{:T(128)}, f32[32,32768]{1,0:T(8,128)}, s32[]{:T(128)}, ...), condition=%wide.region_1.2_spmd, body=%wide.region_0.1_spmd.sunk | while | flops 1343228672 | bytes 48239480 | solution.py:68
  81.0 0.6 compare_convert_fusion.4
  81.7 3.4 fusion.60
  85.1 4.7 copy.62
  89.9 7.1 %convolution_add_fusion.6 = f32[32,32768]{1,0:T(8,128)} fusion(f32[32,32768]{1,0:T(8,128)} %get-tuple-element.390, f32[64,32768]{1,0:T(8,128)S(1)} %bitcast.118, f32[64,8]{0,1:T(8,128)S(1)} %get-tuple-element.404, f32[64,4]{0,1:T(4,128)S(1)} %fusion.61), kind=kOutput, calls=%fused_computation.2.clone.1 | convolution fusion | flops 806356992 | bytes 16780288 | tf_op jit(solution)/shard_map/while/body/dot_general | solution.py:63
  97.2 5.4 %copy.58 = f32[4,8,128,256]{3,2,1,0:T(8,128)} copy(f32[4,8,128,256]{3,1,2,0:T(8,128)} %bitcast.125) | data formatting | bytes 8388608
  102.6 0.0 all-gather.2.cloned.1.call-update
  102.6 0.0 copy-done
  102.6 0.9 copy-done.3
  103.5 2.7 convolution_bitcast_fusion.1
  106.2 5.5 %copy.50 = f32[4,8,128,256]{3,1,2,0:T(8,128)} copy(f32[4,8,128,256]{2,3,0,1:T(8,128)} %convolution_bitcast_fusion.1) | data formatting | bytes 8388608
  111.7 5.0 %broadcast_in_dim.5 = f32[64,32768]{1,0:T(8,128)} broadcast(f32[]{:T(128)} %constant.52.clone.1), dimensions={} | broadcast | bytes 8388612 | tf_op jit(solution)/shard_map/broadcast_in_dim | solution.py:98
  116.7 38.5 %while.25 = (s32[]{:T(128)}, f32[64,32768]{1,0:T(8,128)}, s32[]{:T(128)}, s32[1,1,64]{2,1,0:T(1,128)S(1)}, s32[1,1,64]{2,1,0:T(1,128)S(1)}, /*index=5*/s32[]{:T(...) while((s32[]{:T(128)}, f32[64,32768]{1,0:T(8,128)}, ...), condition=%wide.region_4.5_spmd, body=%wide.region_3.4_spmd.sunk | while | flops 2956991232 | bytes 73405568 | solution.py:99
  116.7 0.7 compare_convert_fusion.5
  117.3 8.8 %convolution_convert_fusion.2 = bf16[64,32768]{1,0:T(8,128)(2,1)S(1)} fusion(f32[32,32768]{1,0:T(8,128)} %get-tuple-element.438, f32[64,8]{0,1:T(8,128)S(1)} %get-tuple-element.437, f32[64,4]{0,1:T(4,128)S(1)} %fusion.67), kind=kOutput, calls=%fused_computation.11.clone.1 | convolution fusion | flops 807405568 | bytes 8391680 | tf_op jit(solution)/shard_map/while/body/dot_general | solution.py:88
  126.2 1.1 copy.63
  127.3 4.6 convolution_bitcast_fusion.4
  131.8 9.2 %copy.64 = f32[8,8,128,256]{3,1,2,0:T(8,128)} copy(f32[8,8,128,256]{2,3,1,0:T(8,128)} %bitcast.120) | data formatting | bytes 16777216 | tf_op jit(solution)/shard_map/while
  141.1 14.1 %convolution_add_fusion.7 = f32[64,32768]{1,0:T(8,128)} fusion(f32[64,32768]{1,0:T(8,128)} %get-tuple-element.421, f32[64,32768]{1,0:T(8,128)} %bitcast.119, s32[64]{0:T(128)S(1)} %bitcast.136), kind=kOutput, calls=%fused_computation.10.clone.1 | convolution fusion | flops 1612713984 | bytes 25166080 | tf_op jit(solution)/shard_map/while/body/dot_general | solution.py:94
  155.2 10.7 %reshape.237 = f32[32,2,32768]{2,1,0:T(2,128)} reshape(f32[64,32768]{1,0:T(8,128)} %get-tuple-element.236) | data formatting | bytes 16777216 | tf_op jit(solution)/shard_map/reshape | solution.py:101
  165.9 7.2 %all-to-all-start.1 = ((f32[32,2,32768]{2,1,0:T(2,128)}), f32[32,2,32768]{2,1,0:T(2,128)}, u32[]{:S(2)}, u32[]{:S(2)}) async-start(f32[32,2,32768]{2,1,0:T(2,128)} %reshape.237), calls=%async_computation.1 | async-start | bytes 16777216 | tf_op jit(solution)/shard_map/all_to_all | solution.py:100
  173.1 0.0 all-reduce.4.cloned.1.call-start
  173.1 0.0 copy-done.8
  173.1 0.1 copy.39
  173.2 0.1 eq.116
  173.3 106.9 %all-to-all-done.1 = f32[32,2,32768]{2,1,0:T(2,128)} async-done(((f32[32,2,32768]{2,1,0:T(2,128)}), f32[32,2,32768]{2,1,0:T(2,128)}, u32[]{:S(2)}, u32[]{:S(2)}) %all-to-all-start.1) | async-done | bytes 8388640 | tf_op jit(solution)/shard_map/all_to_all | solution.py:100
  280.3 10.9 %reshape.238 = f32[64,32768]{1,0:T(8,128)} reshape(f32[32,2,32768]{2,1,0:T(2,128)} %all-to-all-done.1) | data formatting | bytes 16777216 | tf_op jit(solution)/shard_map/reshape | solution.py:110
  291.2 6.2 %fusion.20 = f32[4,32768]{1,0:T(4,128)S(1)} fusion(f32[64,32768]{1,0:T(8,128)} %reshape.238, s32[64]{0:T(128)S(1)} %eq.116), kind=kOutput, calls=%fused_computation.40 | convolution fusion | flops 100663552 | bytes 8913152 | tf_op jit(solution)/shard_map/dot_general | solution.py:110
  297.4 1.2 reshape.239
  298.5 0.0 all-reduce.4.cloned.1.call-update
  298.6 0.0 all-reduce.6.cloned.1.call-start
  298.6 0.0 copy-done.2
  298.6 1.0 fusion.24
  299.6 9.8 %reduce_sum.9 = f32[4,8,128,256]{3,2,1,0:T(8,128)} reduce(f32[4,4,8,128,256]{4,3,2,1,0:T(8,128)} %all-gather.2.cloned.1.call-done, f32[]{:T(128)} %constant.52.clone.1), dimensions={0}, to_apply=%region_2.3 | reduce | flops 3145728 | bytes 20971524 | tf_op jit(solution)/shard_map/reduce_sum | solution.py:77
  309.4 7.0 %convolution_bitcast_fusion.2 = f32[8,256,256]{2,1,0:T(8,128)} fusion(f32[4,8,128,256]{3,2,1,0:T(8,128)} %reduce_sum.9, bf16[4,128,256,1]{2,1,3,0:T(8,128)(2,1)S(1)} %bitcast.133), kind=kOutput, calls=%fused_computation.26 | convolution fusion | flops 3221225472 | bytes 6553600 | tf_op jit(solution)/shard_map/lbnf,lng->bfg/dot_general | solution.py:79
  316.4 0.0 all-reduce.6.cloned.1.call-update
  316.4 37.4 %all-reduce.4.cloned.1.call-done = f32[512,256]{1,0:T(8,128)} async-done(((f32[512,256]{1,0:T(8,128)}), f32[512,256]{1,0:T(8,128)}) %all-reduce.4.cloned.1.call-update) | async-done | bytes 524304 | tf_op jit(solution)/shard_map/psum | solution.py:111
  353.8 0.0 copy-done.4
  353.8 2.1 convolution_add_fusion.2
  355.9 4.6 copy.37
  360.6 3.0 fusion.13
  363.6 0.9 fusion.16
  364.5 103.8 %all-reduce.6.cloned.1.call-done = (f32[8,256,256]{2,1,0:T(8,128)}, f32[256,256]{1,0:T(8,128)}) async-done(((f32[8,256,256]{2,1,0:T(8,128)}, f32[256,256]{1,0:T(8,128)}), (f32[8,256,256]{2,1,0:T(8,128)}, f32[256,256]{1,0:T(8,128)})) %all-reduce.6.cloned.1.call-update) | async-done | bytes 2359312 | tf_op jit(solution)/shard_map/psum | solution.py:80
  468.4 3.1 copy.82
  471.4 0.0 copy-done.5
  471.4 0.7 copy.83
  (14 shorter events, 0.0 us)
Async XLA Ops:
  7.2 95.4 %copy-start = (bf16[8,256,256]{2,1,0:T(8,128)(2,1)S(1)}, bf16[8,256,256]{2,1,0:T(8,128)(2,1)}, u32[]{:S(2)}) copy-start(bf16[8,256,256]{2,1,0:T(8,128)(2,1)} %param.16) | copy-start | bytes 3145732
  11.9 10.3 %copy-start.7 = (s32[1,1,64]{2,1,0:T(1,128)S(1)}, s32[1,1,64]{2,1,0:T(1,128)}, u32[]{:S(2)}) copy-start(s32[1,1,64]{2,1,0:T(1,128)} %param.21) | copy-start | bytes 772
  11.9 10.4 %copy-start.9 = (f32[200,8]{0,1:T(8,128)S(1)}, f32[200,8]{0,1:T(8,128)}, u32[]{:S(2)}) copy-start(f32[200,8]{0,1:T(8,128)} %param.18) | copy-start | bytes 19204
  11.9 10.4 %copy-start.10 = (s32[1,1,64]{2,1,0:T(1,128)S(1)}, s32[1,1,64]{2,1,0:T(1,128)}, u32[]{:S(2)}) copy-start(s32[1,1,64]{2,1,0:T(1,128)} %param.22) | copy-start | bytes 772
  11.9 61.7 %all-to-all-start = ((bf16[32,2,128,256]{3,2,1,0:T(8,128)(2,1)}), bf16[32,2,128,256]{3,2,1,0:T(8,128)(2,1)}, u32[]{:S(2)}, u32[]{:S(2)}) async-start(bf16[32,2,128,256]{3,2,1,0:T(8,128)(2,1)} %bitcast.130), calls=%async_computation | async-start | bytes 8388608 | tf_op jit(solution)/shard_map/all_to_all | solution.py:39
  21.5 278.1 %all-gather.2.cloned.1.call-start = ((), (), s32[]{:S(2)}) async-start(), calls=%async_computation.2 | async-start | bytes 20971520 | tf_op jit(solution)/shard_map/all_gather | solution.py:77
  78.6 2.4 copy-start.1
  78.6 2.4 copy-start.6
  102.6 0.9 copy-start.3
  165.9 7.3 %copy-start.8 = (s32[1,1,32,2]{2,3,1,0:T(2,128)S(1)}, s32[1,1,32,2]{2,3,1,0:T(2,128)}, u32[]{:S(2)}) copy-start(s32[1,1,32,2]{2,3,1,0:T(2,128)} %param.24) | copy-start | bytes 772
  165.9 114.4 %all-to-all-start.1 = ((f32[32,2,32768]{2,1,0:T(2,128)}), f32[32,2,32768]{2,1,0:T(2,128)}, u32[]{:S(2)}, u32[]{:S(2)}) async-start(f32[32,2,32768]{2,1,0:T(2,128)} %reshape.237), calls=%async_computation.1 | async-start | bytes 16777216 | tf_op jit(solution)/shard_map/all_to_all | solution.py:100
  173.1 180.8 %all-reduce.4.cloned.1.call-start = ((), (), s32[]{:S(2)}) async-start(), calls=%async_computation.3 | async-start | bytes 1048576 | tf_op jit(solution)/shard_map/psum | solution.py:111
  291.2 7.4 %copy-start.2 = (bf16[512,256]{1,0:T(8,128)(2,1)S(1)}, bf16[512,256]{1,0:T(8,128)(2,1)}, u32[]{:S(2)}) copy-start(bf16[512,256]{1,0:T(8,128)(2,1)} %param.15) | copy-start | bytes 786436
  298.6 169.8 %all-reduce.6.cloned.1.call-start = ((), (), s32[]{:S(2)}) async-start(), calls=%async_computation.4 | async-start | bytes 4718592 | tf_op jit(solution)/shard_map/psum | solution.py:80
  309.4 44.4 %copy-start.4 = (bf16[256,256]{1,0:T(8,128)(2,1)S(1)}, bf16[256,256]{1,0:T(8,128)(2,1)}, u32[]{:S(2)}) copy-start(bf16[256,256]{1,0:T(8,128)(2,1)} %param.17) | copy-start | bytes 393220
  468.3 3.1 copy-start.5
Sparse Core Ops, SparseCore 0:
  102.7 154.6 all-gather.1
  298.7 55.1 all-reduce.3
  357.8 110.4 all-reduce.5
